TPU v7x, 32 devices: a whole 2x2x4 slice. The times are simulated.
32 devices in a mesh: row: 4 (over z), col: 8 (over y, x, core).
Axes of the slice: x: 2, y: 2, z: 4, core: 2. Of those that a mesh axis runs over, the one named last changes fastest.
Arguments:
- inputs: bfloat16 [192, 12288], P('col', 'row'), may hold values from -40 to 40
- ln_gain: float32 [12288], P('row'), may hold values from 0.25 to 1.75
- ln_bias: float32 [12288], P('row'), may hold values from -4 to 4
- w_up: bfloat16 [12288, 49152], P('row', 'col'), may hold values from -0.0546875 to 0.0546875
- up_bias: float32 [49152], P('col'), may hold values from -4 to 4
- w_down: bfloat16 [49152, 12288], P('col', 'row'), may hold values from -0.02734375 to 0.02734375
- down_bias: float32 [12288], P('row'), may hold values from -4 to 4
Outputs:
- block_out: bfloat16 [192, 12288], P('col', 'row')
All inputs are finite; a program needn't handle non-finite values.
Results may differ from a plain program's by a relative error of at most 0.0085.
Values may be sent and summed in bfloat16 or wider, within the bound.
No kernel may reach another device: no remote copies, remote signals or barrier semaphores. Data moves between devices by JAX's collectives and lax.ppermute only.
A program may use at most 128 MiB of HBM per device.

v0:
```python
import jax
import jax.numpy as jnp
from jax import lax
from jax.sharding import PartitionSpec as P

D = 12288


def local(inputs, ln_gain, ln_bias, w_up, up_bias, w_down, down_bias):
    in_float = inputs.astype(jnp.float32)
    total, squares = lax.psum(
        (jnp.sum(in_float, axis=1), jnp.sum(in_float * in_float, axis=1)), "row"
    )
    average = total / D
    centered = in_float - average[:, None]
    variance = squares / D - average * average
    normed = (centered * lax.rsqrt(variance + 1e-05)[:, None] * ln_gain + ln_bias).astype(
        jnp.bfloat16
    )
    gathered = lax.all_gather(normed, "col", axis=0, tiled=True)
    summed = lax.psum_scatter(
        jnp.dot(gathered, w_up, preferred_element_type=jnp.float32).astype(jnp.bfloat16),
        "row",
        scatter_dimension=0,
        tiled=True,
    ).astype(jnp.float32)
    hidden = jax.nn.gelu(summed + up_bias, approximate=True).astype(jnp.bfloat16)
    terms = jnp.dot(
        lax.all_gather(hidden, "row", axis=0, tiled=True),
        w_down,
        preferred_element_type=jnp.float32,
    )
    down_sum = lax.psum_scatter(
        terms.astype(jnp.bfloat16), "col", scatter_dimension=0, tiled=True
    ).astype(jnp.float32)
    return (in_float + down_sum + down_bias).astype(jnp.bfloat16)


def solution(mesh):
    placed = (
        P("col", "row"),
        P("row"),
        P("row"),
        P("row", "col"),
        P("col"),
        P("col", "row"),
        P("row"),
    )
    return jax.shard_map(
        local, mesh=mesh, in_specs=placed, out_specs=P("col", "row"), check_vma=False
    )
```

profile of v0, /device:TPU:0, one launch (start us, length us, event | category | flops | bytes accessed | tf_op | source)
XLA Modules:
  0.0 223.3 jit_solution(8975903873406821275)
XLA Ops:
  6.5 0.0 all-gather.3.cloned.1.call-start
  6.5 1.1 convert_reduce_fusion
  7.6 13.5 %all-reduce = (f32[24]{0:T(128)S(1)}, f32[24]{0:T(128)S(1)}) all-reduce(f32[24]{0:T(128)S(1)} %get-tuple-element.6, f32[24]{0:T(128)S(1)} %get-tuple-element.5), channel_id=1, replica_groups=mesh['row'=4,'col'=8] {'row'}, use_global_device_ids=true, to_apply=%region_3.0 | all-reduce | flops 48 | bytes 384 | tf_op jit(solution)/shard_map/psum | solution.py:11
  21.1 1.7 fusion.11
  22.8 0.0 all-gather.3.cloned.1.call-update
  22.8 0.0 reduce-scatter.3.cloned.1.call-start
  22.9 22.2 %all-gather.3.cloned.1.call-done = bf16[192,3072]{1,0:T(8,128)(2,1)} async-done(((bf16[24,3072]{1,0:T(8,128)(2,1)}), bf16[192,3072]{1,0:T(8,128)(2,1)}) %all-gather.3.cloned.1.call-update) | async-done | bytes 1179664 | tf_op jit(solution)/shard_map/all_gather | solution.py:20
  45.1 17.4 %convolution_convert_fusion = bf16[192,6144]{1,0:T(8,128)(2,1)} fusion(bf16[192,3072]{1,0:T(8,128)(2,1)} %all-gather.3.cloned.1.call-done, bf16[3072,6144]{1,0:T(8,128)(2,1)} %param.10), kind=kOutput, calls=%fused_computation | convolution fusion | flops 7248936960 | bytes 41287680 | tf_op jit(solution)/shard_map/dot_general | solution.py:22
  62.5 0.0 copy-start.1
  62.5 0.0 reduce-scatter.3.cloned.1.call-update
  62.5 0.0 all-gather.5.cloned.1.call-start
  62.5 47.8 %reduce-scatter.3.cloned.1.call-done = bf16[48,6144]{1,0:T(8,128)(2,1)} async-done(((bf16[192,6144]{1,0:T(8,128)(2,1)}), bf16[48,6144]{1,0:T(8,128)(2,1)}) %reduce-scatter.3.cloned.1.call-update) | async-done | bytes 589840 | tf_op jit(solution)/shard_map/reduce_scatter | solution.py:21
  110.4 0.0 copy-done.1
  110.4 2.3 %fusion.7 = bf16[48,6144]{1,0:T(8,128)(2,1)} fusion(bf16[48,6144]{1,0:T(8,128)(2,1)} %reduce-scatter.3.cloned.1.call-done, f32[6144]{0:T(1024)S(1)} %copy-done.1), kind=kLoop, calls=%fused_computation.10 | loop fusion | flops 3244032 | bytes 1204224 | tf_op jit(solution)/shard_map/convert_element_type | solution.py:27
  112.7 0.0 all-gather.5.cloned.1.call-update
  112.7 0.0 reduce-scatter.5.cloned.1.call-start
  112.8 49.5 %all-gather.5.cloned.1.call-done = bf16[192,6144]{1,0:T(8,128)(2,1)} async-done(((bf16[48,6144]{1,0:T(8,128)(2,1)}), bf16[192,6144]{1,0:T(8,128)(2,1)}) %all-gather.5.cloned.1.call-update) | async-done | bytes 2359312 | tf_op jit(solution)/shard_map/all_gather | solution.py:29
  162.2 17.3 %convolution_convert_fusion.1 = bf16[192,3072]{1,0:T(8,128)(2,1)} fusion(bf16[192,6144]{1,0:T(8,128)(2,1)} %all-gather.5.cloned.1.call-done, bf16[6144,3072]{1,0:T(8,128)(2,1)} %param.12), kind=kOutput, calls=%fused_computation.1 | convolution fusion | flops 7248347136 | bytes 41287680 | tf_op jit(solution)/shard_map/dot_general | solution.py:28
  179.5 0.0 copy-start
  179.5 0.0 copy-start.2
  179.5 0.0 reduce-scatter.5.cloned.1.call-update
  179.5 35.6 %reduce-scatter.5.cloned.1.call-done = bf16[24,3072]{1,0:T(8,128)(2,1)} async-done(((bf16[192,3072]{1,0:T(8,128)(2,1)}), bf16[24,3072]{1,0:T(8,128)(2,1)}) %reduce-scatter.5.cloned.1.call-update) | async-done | bytes 147472 | tf_op jit(solution)/shard_map/reduce_scatter | solution.py:33
  215.1 0.0 copy-done
  215.1 0.0 copy-done.2
  215.1 1.6 fusion.14
  (1 shorter events, 0.0 us)
Async XLA Ops:
  6.5 38.6 %all-gather.3.cloned.1.call-start = ((), (), s32[]{:S(2)}) async-start(), calls=%async_computation.2 | async-start | bytes 1327104 | tf_op jit(solution)/shard_map/all_gather | solution.py:20
  22.8 87.5 %reduce-scatter.3.cloned.1.call-start = ((), (), s32[]{:S(2)}) async-start(), calls=%async_computation.3 | async-start | bytes 2949120 | tf_op jit(solution)/shard_map/reduce_scatter | solution.py:21
  62.5 47.9 %copy-start.1 = (f32[6144]{0:T(1024)S(1)}, f32[6144]{0:T(1024)}, u32[]{:S(2)}) copy-start(f32[6144]{0:T(1024)} %param.11) | copy-start | bytes 73732
  62.5 99.7 %all-gather.5.cloned.1.call-start = ((), (), s32[]{:S(2)}) async-start(), calls=%async_computation.4 | async-start | bytes 2949120 | tf_op jit(solution)/shard_map/all_gather | solution.py:29
  112.7 102.4 %reduce-scatter.5.cloned.1.call-start = ((), (), s32[]{:S(2)}) async-start(), calls=%async_computation.5 | async-start | bytes 1327104 | tf_op jit(solution)/shard_map/reduce_scatter | solution.py:33
  179.5 35.6 %copy-start = (bf16[24,3072]{1,0:T(8,128)(2,1)S(1)}, bf16[24,3072]{1,0:T(8,128)(2,1)}, u32[]{:S(2)}) copy-start(bf16[24,3072]{1,0:T(8,128)(2,1)} %param.7) | copy-start | bytes 442372
  179.5 35.6 %copy-start.2 = (f32[3072]{0:T(1024)S(1)}, f32[3072]{0:T(1024)}, u32[]{:S(2)}) copy-start(f32[3072]{0:T(1024)} %param.13) | copy-start | bytes 36868
Sparse Core Ops, SparseCore 0:
  22.9 22.1 all-gather.2
  62.6 47.6 reduce-scatter.2
  112.8 49.3 all-gather.4
  179.6 35.4 reduce-scatter.4
where the time goes:
time: 224 us; the launch traced here: 223 us
  waiting for transfers between devices  155 us (69%)
  matrix products  34.6 us (15%)
  blocking collectives  13.5 us (6%)
  between operations  13.1 us (6%)
  other arithmetic  6.73 us (3%)
    all_gather x1, waiting for transfers between devices, local(): lax.all_gather(hidden, 'row', axis=0, tiled=True)  49.5 us
    reduce_scatter x1, waiting for transfers between devices, local(): lax.psum_scatter(jnp.dot(gathered, w_up, preferred_element_type=jnp.float...  47.8 us
    reduce_scatter x1, waiting for transfers between devices, local(): lax.psum_scatter(terms.astype(jnp.bfloat16), 'col', scatter_dimension=0,...  35.6 us
    all_gather x1, waiting for transfers between devices, local(): gathered = lax.all_gather(normed, 'col', axis=0, tiled=True)  22.2 us
    dot_general x1, matrix products, local(): jnp.dot(gathered, w_up, preferred_element_type=jnp.float32)  17.4 us
    dot_general x1, matrix products, local(): jnp.dot(lax.all_gather(hidden, 'row', axis=0, tiled=True), w_down, prefer...  17.3 us
    psum x1, blocking collectives, local(): lax.psum((jnp.sum(in_float, axis=1), jnp.sum(in_float * in_float, axis=1)...  13.5 us
  transfers between devices with their start and end apart: 4, of which 4 were waited for; matrix products, arithmetic and copies ran while one was open for 0% of the time, Pallas kernels for 0%

commit v1 on v0

--- a/solution.py
+++ b/solution.py
@@ -17,7 +17,12 @@
     normed = (centered * lax.rsqrt(variance + 1e-05)[:, None] * ln_gain + ln_bias).astype(
         jnp.bfloat16
     )
-    gathered = lax.all_gather(normed, "col", axis=0, tiled=True)
+    ring = [normed]
+    for hop in range(7):
+        ring.append(lax.ppermute(ring[-1], "col", [(dev, (dev + 1) % 8) for dev in range(8)]))
+    gathered = jnp.roll(
+        jnp.concatenate(ring[::-1], axis=0), (lax.axis_index("col") + 1) * ring[0].shape[0], axis=0
+    )
     summed = lax.psum_scatter(
         jnp.dot(gathered, w_up, preferred_element_type=jnp.float32).astype(jnp.bfloat16),
         "row",

time: 224 us -> 236 us (1.054)
  waiting for transfers between devices: 155 us -> 168 us
    ppermute x0 -> x7, waiting for transfers between devices: none -> 38.2 us  [local(): lax.ppermute(ring[-1], 'col', [(dev, (dev + 1) % 8) for dev in range(8)])]
    all_gather x1 -> x0, waiting for transfers between devices: 22.2 us -> none  [local(): gathered = lax.all_gather(normed, 'col', axis=0, tiled=True)]
    reduce_scatter x1, waiting for transfers between devices: 47.8 us -> 45.1 us  [local(): lax.psum_scatter(jnp.dot(gathered, w_up, preferred_element_type=jnp.float...]
  transfers between devices with their start and end apart: 4 -> 10, of which waited for: 4 -> 10; matrix products, arithmetic and copies ran while one was open for 0% -> 0% of each run, Pallas kernels for 0% -> 0%
where the time goes in v1:
time: 236 us
  waiting for transfers between devices  168 us (71%)
  matrix products  33.7 us (14%)
  blocking collectives  13.5 us (6%)
  between operations  13.3 us (6%)
  other arithmetic  6.37 us (3%)
    all_gather x1, waiting for transfers between devices, local(): lax.all_gather(hidden, 'row', axis=0, tiled=True)  49.5 us
    reduce_scatter x1, waiting for transfers between devices, local(): lax.psum_scatter(jnp.dot(gathered, w_up, preferred_element_type=jnp.float...  45.1 us
    ppermute x7, waiting for transfers between devices, local(): lax.ppermute(ring[-1], 'col', [(dev, (dev + 1) % 8) for dev in range(8)])  38.2 us
    reduce_scatter x1, waiting for transfers between devices, local(): lax.psum_scatter(terms.astype(jnp.bfloat16), 'col', scatter_dimension=0,...  35.6 us
    dot_general x1, matrix products, local(): jnp.dot(lax.all_gather(hidden, 'row', axis=0, tiled=True), w_down, prefer...  17.3 us
    dot_general x1, matrix products, local(): jnp.dot(gathered, w_up, preferred_element_type=jnp.float32)  16.4 us
    psum x1, blocking collectives, local(): lax.psum((jnp.sum(in_float, axis=1), jnp.sum(in_float * in_float, axis=1)...  13.5 us
  transfers between devices with their start and end apart: 10, of which 10 were waited for; matrix products, arithmetic and copies ran while one was open for 0% of the time, Pallas kernels for 0%

profile of v1, /device:TPU:0, one launch (start us, length us, event | category | flops | bytes accessed | tf_op | source)
XLA Modules:
  0.0 235.6 jit_solution(8484304511726947115)
XLA Ops:
  6.5 0.0 copy-start
  6.5 0.0 copy-start.2
  6.5 0.0 copy-start.1
  6.5 0.0 reduce-scatter.3.cloned.1.call-start
  6.5 1.1 convert_reduce_fusion
  7.7 13.5 %all-reduce = (f32[24]{0:T(128)S(1)}, f32[24]{0:T(128)S(1)}) all-reduce(f32[24]{0:T(128)S(1)} %get-tuple-element.6, f32[24]{0:T(128)S(1)} %get-tuple-element.5), channel_id=1, replica_groups=mesh['row'=4,'col'=8] {'row'}, use_global_device_ids=true, to_apply=%region_3.0 | all-reduce | flops 48 | bytes 384 | tf_op jit(solution)/shard_map/psum | solution.py:11
  21.2 1.1 fusion.12
  22.2 0.1 collective-permute-start
  22.3 5.5 %collective-permute-done = bf16[24,3072]{1,0:T(8,128)(2,1)S(1)} collective-permute-done((bf16[24,3072]{1,0:T(8,128)(2,1)S(1)}, bf16[24,3072]{1,0:T(8,128)(2,1)S(1)}, u32[]{:S(2)}, u32[]{:S(2)}) %collective-permute-start) | collective-permute-done | bytes 147488 | tf_op jit(solution)/shard_map/ppermute | solution.py:22
  27.7 0.0 collective-permute-start.1
  27.7 5.5 %collective-permute-done.1 = bf16[24,3072]{1,0:T(8,128)(2,1)S(1)} collective-permute-done((bf16[24,3072]{1,0:T(8,128)(2,1)S(1)}, bf16[24,3072]{1,0:T(8,128)(2,1)S(1)}, u32[]{:S(2)}, u32[]{:S(2)}) %collective-permute-start.1) | collective-permute-done | bytes 147488 | tf_op jit(solution)/shard_map/ppermute | solution.py:22
  33.2 0.0 collective-permute-start.2
  33.2 5.5 %collective-permute-done.2 = bf16[24,3072]{1,0:T(8,128)(2,1)S(1)} collective-permute-done((bf16[24,3072]{1,0:T(8,128)(2,1)S(1)}, bf16[24,3072]{1,0:T(8,128)(2,1)S(1)}, u32[]{:S(2)}, u32[]{:S(2)}) %collective-permute-start.2) | collective-permute-done | bytes 147488 | tf_op jit(solution)/shard_map/ppermute | solution.py:22
  38.7 0.0 collective-permute-start.3
  38.7 5.5 %collective-permute-done.3 = bf16[24,3072]{1,0:T(8,128)(2,1)S(1)} collective-permute-done((bf16[24,3072]{1,0:T(8,128)(2,1)S(1)}, bf16[24,3072]{1,0:T(8,128)(2,1)S(1)}, u32[]{:S(2)}, u32[]{:S(2)}) %collective-permute-start.3) | collective-permute-done | bytes 147488 | tf_op jit(solution)/shard_map/ppermute | solution.py:22
  44.1 0.0 collective-permute-start.4
  44.1 5.5 %collective-permute-done.4 = bf16[24,3072]{1,0:T(8,128)(2,1)S(1)} collective-permute-done((bf16[24,3072]{1,0:T(8,128)(2,1)S(1)}, bf16[24,3072]{1,0:T(8,128)(2,1)S(1)}, u32[]{:S(2)}, u32[]{:S(2)}) %collective-permute-start.4) | collective-permute-done | bytes 147488 | tf_op jit(solution)/shard_map/ppermute | solution.py:22
  49.6 0.0 collective-permute-start.5
  49.6 5.5 %collective-permute-done.5 = bf16[24,3072]{1,0:T(8,128)(2,1)S(1)} collective-permute-done((bf16[24,3072]{1,0:T(8,128)(2,1)S(1)}, bf16[24,3072]{1,0:T(8,128)(2,1)S(1)}, u32[]{:S(2)}, u32[]{:S(2)}) %collective-permute-start.5) | collective-permute-done | bytes 147488 | tf_op jit(solution)/shard_map/ppermute | solution.py:22
  55.1 0.0 collective-permute-start.6
  55.1 5.5 %collective-permute-done.6 = bf16[24,3072]{1,0:T(8,128)(2,1)S(1)} collective-permute-done((bf16[24,3072]{1,0:T(8,128)(2,1)S(1)}, bf16[24,3072]{1,0:T(8,128)(2,1)S(1)}, u32[]{:S(2)}, u32[]{:S(2)}) %collective-permute-start.6) | collective-permute-done | bytes 147488 | tf_op jit(solution)/shard_map/ppermute | solution.py:22
  60.7 0.0 copy-done
  60.7 0.0 copy-done.2
  60.7 0.0 copy-done.1
  60.7 0.1 constant_dynamic-update-slice_fusion.8
  61.0 0.1 constant_dynamic-update-slice_fusion
  61.1 16.4 %convolution_convert_fusion = bf16[192,6144]{1,0:T(8,128)(2,1)} fusion(bf16[3072,6144]{1,0:T(8,128)(2,1)} %param.10, bf16[384,3072]{1,0:T(8,128)(2,1)S(1)} %constant_dynamic-update-slice_fusion, s32[]{:T(128)S(6)} %select_n.14), kind=kOutput, calls=%fused_computation | convolution fusion | flops 7248936960 | bytes 41287684 | tf_op jit(solution)/shard_map/dot_general | solution.py:27
  77.5 0.0 copy-start.3
  77.5 0.0 reduce-scatter.3.cloned.1.call-update
  77.5 0.0 all-gather.2.cloned.1.call-start
  77.6 45.1 %reduce-scatter.3.cloned.1.call-done = bf16[48,6144]{1,0:T(8,128)(2,1)} async-done(((bf16[192,6144]{1,0:T(8,128)(2,1)}), bf16[48,6144]{1,0:T(8,128)(2,1)}) %reduce-scatter.3.cloned.1.call-update) | async-done | bytes 589840 | tf_op jit(solution)/shard_map/reduce_scatter | solution.py:26
  122.7 0.0 copy-done.3
  122.7 2.3 fusion.7
  125.0 0.0 all-gather.2.cloned.1.call-update
  125.0 0.0 copy-start.4
  125.0 0.0 reduce-scatter.5.cloned.1.call-start
  125.1 49.5 %all-gather.2.cloned.1.call-done = bf16[192,6144]{1,0:T(8,128)(2,1)} async-done(((bf16[48,6144]{1,0:T(8,128)(2,1)}), bf16[192,6144]{1,0:T(8,128)(2,1)}) %all-gather.2.cloned.1.call-update) | async-done | bytes 2359312 | tf_op jit(solution)/shard_map/all_gather | solution.py:34
  174.5 17.3 %convolution_convert_fusion.1 = bf16[192,3072]{1,0:T(8,128)(2,1)} fusion(bf16[192,6144]{1,0:T(8,128)(2,1)} %all-gather.2.cloned.1.call-done, bf16[6144,3072]{1,0:T(8,128)(2,1)} %param.12), kind=kOutput, calls=%fused_computation.1 | convolution fusion | flops 7248347136 | bytes 41287680 | tf_op jit(solution)/shard_map/dot_general | solution.py:33
  191.8 0.0 reduce-scatter.5.cloned.1.call-update
  191.8 35.6 %reduce-scatter.5.cloned.1.call-done = bf16[24,3072]{1,0:T(8,128)(2,1)} async-done(((bf16[192,3072]{1,0:T(8,128)(2,1)}), bf16[24,3072]{1,0:T(8,128)(2,1)}) %reduce-scatter.5.cloned.1.call-update) | async-done | bytes 147472 | tf_op jit(solution)/shard_map/reduce_scatter | solution.py:38
  227.4 0.0 copy-done.4
  227.4 1.6 fusion.15
  (15 shorter events, 0.2 us)
Async XLA Ops:
  6.5 54.1 %copy-start = (bf16[24,3072]{1,0:T(8,128)(2,1)S(1)}, bf16[24,3072]{1,0:T(8,128)(2,1)}, u32[]{:S(2)}) copy-start(bf16[24,3072]{1,0:T(8,128)(2,1)} %param.7) | copy-start | bytes 442372
  6.5 54.2 %copy-start.2 = (f32[3072]{0:T(1024)S(1)}, f32[3072]{0:T(1024)}, u32[]{:S(2)}) copy-start(f32[3072]{0:T(1024)} %param.8) | copy-start | bytes 36868
  6.5 54.2 %copy-start.1 = (f32[3072]{0:T(1024)S(1)}, f32[3072]{0:T(1024)}, u32[]{:S(2)}) copy-start(f32[3072]{0:T(1024)} %param.9) | copy-start | bytes 36868
  6.5 116.1 %reduce-scatter.3.cloned.1.call-start = ((), (), s32[]{:S(2)}) async-start(), calls=%async_computation.2 | async-start | bytes 2949120 | tf_op jit(solution)/shard_map/reduce_scatter | solution.py:26
  22.2 5.5 %collective-permute-start = (bf16[24,3072]{1,0:T(8,128)(2,1)S(1)}, bf16[24,3072]{1,0:T(8,128)(2,1)S(1)}, u32[]{:S(2)}, u32[]{:S(2)}) collective-permute-start(bf16[24,3072]{1,0:T(8,128)(2,1)S(1)} %fusion.12), channel_id=1, source_target_pairs={{0,1},{1,2},{2,3},{3,4},{4,5},{5,6},{6,7},{7,0},{8,9},{9,10},{10,1... | collective-permute-start | bytes 442376 | tf_op jit(solution)/shard_map/ppermute | solution.py:22
  27.7 5.5 %collective-permute-start.1 = (bf16[24,3072]{1,0:T(8,128)(2,1)S(1)}, bf16[24,3072]{1,0:T(8,128)(2,1)S(1)}, u32[]{:S(2)}, u32[]{:S(2)}) collective-permute-start(bf16[24,3072]{1,0:T(8,128)(2,1)S(1)} %collective-permute-done), channel_id=1, source_target_pairs={{0,1},{1,2},{2,3},{3,4},{4,5},{5,6},{6,7},{7,0},{8,9},{9,10},{10,1... | collective-permute-start | bytes 442376 | tf_op jit(solution)/shard_map/ppermute | solution.py:22
  33.2 5.5 %collective-permute-start.2 = (bf16[24,3072]{1,0:T(8,128)(2,1)S(1)}, bf16[24,3072]{1,0:T(8,128)(2,1)S(1)}, u32[]{:S(2)}, u32[]{:S(2)}) collective-permute-start(bf16[24,3072]{1,0:T(8,128)(2,1)S(1)} %collective-permute-done.1), channel_id=1, source_target_pairs={{0,1},{1,2},{2,3},{3,4},{4,5},{5,6},{6,7},{7,0},{8,9},{9,10},{10,1... | collective-permute-start | bytes 442376 | tf_op jit(solution)/shard_map/ppermute | solution.py:22
  38.7 5.5 %collective-permute-start.3 = (bf16[24,3072]{1,0:T(8,128)(2,1)S(1)}, bf16[24,3072]{1,0:T(8,128)(2,1)S(1)}, u32[]{:S(2)}, u32[]{:S(2)}) collective-permute-start(bf16[24,3072]{1,0:T(8,128)(2,1)S(1)} %collective-permute-done.2), channel_id=1, source_target_pairs={{0,1},{1,2},{2,3},{3,4},{4,5},{5,6},{6,7},{7,0},{8,9},{9,10},{10,1... | collective-permute-start | bytes 442376 | tf_op jit(solution)/shard_map/ppermute | solution.py:22
  44.1 5.5 %collective-permute-start.4 = (bf16[24,3072]{1,0:T(8,128)(2,1)S(1)}, bf16[24,3072]{1,0:T(8,128)(2,1)S(1)}, u32[]{:S(2)}, u32[]{:S(2)}) collective-permute-start(bf16[24,3072]{1,0:T(8,128)(2,1)S(1)} %collective-permute-done.3), channel_id=1, source_target_pairs={{0,1},{1,2},{2,3},{3,4},{4,5},{5,6},{6,7},{7,0},{8,9},{9,10},{10,1... | collective-permute-start | bytes 442376 | tf_op jit(solution)/shard_map/ppermute | solution.py:22
  49.6 5.5 %collective-permute-start.5 = (bf16[24,3072]{1,0:T(8,128)(2,1)S(1)}, bf16[24,3072]{1,0:T(8,128)(2,1)S(1)}, u32[]{:S(2)}, u32[]{:S(2)}) collective-permute-start(bf16[24,3072]{1,0:T(8,128)(2,1)S(1)} %collective-permute-done.4), channel_id=1, source_target_pairs={{0,1},{1,2},{2,3},{3,4},{4,5},{5,6},{6,7},{7,0},{8,9},{9,10},{10,1... | collective-permute-start | bytes 442376 | tf_op jit(solution)/shard_map/ppermute | solution.py:22
  55.1 5.5 %collective-permute-start.6 = (bf16[24,3072]{1,0:T(8,128)(2,1)S(1)}, bf16[24,3072]{1,0:T(8,128)(2,1)S(1)}, u32[]{:S(2)}, u32[]{:S(2)}) collective-permute-start(bf16[24,3072]{1,0:T(8,128)(2,1)S(1)} %collective-permute-done.5), channel_id=1, source_target_pairs={{0,1},{1,2},{2,3},{3,4},{4,5},{5,6},{6,7},{7,0},{8,9},{9,10},{10,1... | collective-permute-start | bytes 442376 | tf_op jit(solution)/shard_map/ppermute | solution.py:22
  77.5 45.2 %copy-start.3 = (f32[6144]{0:T(1024)S(1)}, f32[6144]{0:T(1024)}, u32[]{:S(2)}) copy-start(f32[6144]{0:T(1024)} %param.11) | copy-start | bytes 73732
  77.5 97.0 %all-gather.2.cloned.1.call-start = ((), (), s32[]{:S(2)}) async-start(), calls=%async_computation.3 | async-start | bytes 2949120 | tf_op jit(solution)/shard_map/all_gather | solution.py:34
  125.0 102.4 %copy-start.4 = (f32[3072]{0:T(1024)S(1)}, f32[3072]{0:T(1024)}, u32[]{:S(2)}) copy-start(f32[3072]{0:T(1024)} %param.13) | copy-start | bytes 36868
  125.0 102.4 %reduce-scatter.5.cloned.1.call-start = ((), (), s32[]{:S(2)}) async-start(), calls=%async_computation.4 | async-start | bytes 1327104 | tf_op jit(solution)/shard_map/reduce_scatter | solution.py:38
Sparse Core Ops, SparseCore 0:
  77.6 44.9 reduce-scatter.2
  125.1 49.3 all-gather.1
  191.9 35.4 reduce-scatter.4
